TPU v7x, 256 devices: a whole 4x4x8 slice. The times are simulated.
256 devices in a mesh: gx: 8 (over y, z_hi), gy: 8 (over z_lo, core), gz: 4 (over x).
Axes of the slice: x: 4, y: 4, z: 8 (z_hi: 2, z_lo: 4; z = z_hi * 4 + z_lo), core: 2. Of those that a mesh axis runs over, the one named last changes fastest.
Arguments:
- right_side: float32 [3, 64, 64, 512], P(None, 'gx', 'gy', 'gz'), may hold values from -17 to 17
- phase_labels: int32 [32, 32, 256], P('gx', 'gy', 'gz'), may hold values from 0 to 7
- phase_moduli: float32 [8], replicated, may hold values from 0.03 to 0.3
- coarse_nodes: int32 [64, 64, 512], P('gx', 'gy', 'gz'), may hold values from 0 to 5
- coarse_inverse: float32 [9216, 9216], P(('gx', 'gy', 'gz')), as said below
Outputs:
- solution_field: float32 [3, 64, 64, 512], P(None, 'gx', 'gy', 'gz')
- residual: float32 [3, 64, 64, 512], P(None, 'gx', 'gy', 'gz')
Inputs may be any that keep to these rules, and one draw needn't show every extreme that they name: `coarse_inverse`: symmetric.
All inputs are finite; a program needn't handle non-finite values.
Results may differ from a plain program's by a relative error of at most 0.0003.
Values sent between devices are 32-bit elements; how exact they have to be, the bound alone decides.
A program may use at most 64 MiB of HBM per device.

v0:
```python
import jax
import jax.numpy as jnp
from jax import lax
from jax.sharding import PartitionSpec as P

SWEEPS = 4
ITERS = 2
bond_ratio = 0.5
relax = 0.6
highest = lax.Precision.HIGHEST
neighbour_offsets = tuple(
    (
        (shift_x, shift_y, shift_z)
        for shift_x in (-1, 0, 1)
        for shift_y in (-1, 0, 1)
        for shift_z in (-1, 0, 1)
        if shift_x * shift_x + shift_y * shift_y + shift_z * shift_z > 0
    )
)


def extended(x, sides, width):
    for axis, dim in sides:
        size, length = (lax.axis_size(axis), x.shape[dim])
        up = [(i, (i + 1) % size) for i in range(size - 1)]
        down = [(j, i) for i, j in up]
        last = lax.slice_in_dim(x, length - width, length, axis=dim)
        leading = lax.slice_in_dim(x, 0, width, axis=dim)
        before = lax.ppermute(last, axis, up)
        after = lax.ppermute(leading, axis, down)
        x = jnp.concatenate([before, x, after], axis=dim)
    return x


def inner_view(array, shift_x, shift_y, shift_z):
    size_x, size_y, size_z = array.shape[-3:]
    return array[
        ...,
        1 + shift_x : size_x - 1 + shift_x,
        1 + shift_y : size_y - 1 + shift_y,
        1 + shift_z : size_z - 1 + shift_z,
    ]


def spring_force(field_pad, stiff_pad):
    centre = inner_view(field_pad, 0, 0, 0)
    stiff_centre = inner_view(stiff_pad, 0, 0, 0)
    parts = [jnp.zeros_like(centre[0]) for component in range(3)]
    for offset in neighbour_offsets:
        length = offset[0] * offset[0] + offset[1] * offset[1] + offset[2] * offset[2]
        spring = (
            0.5 * (stiff_centre + inner_view(stiff_pad, offset[0], offset[1], offset[2])) / length
        )
        partner = inner_view(field_pad, offset[0], offset[1], offset[2])
        stretch = [centre[component] - partner[component] for component in range(3)]
        projected = jnp.zeros_like(stretch[0])
        for component in range(3):
            if offset[component] != 0:
                projected = projected + offset[component] * stretch[component]
        for component in range(3):
            summand = stretch[component]
            if offset[component] != 0:
                summand = summand + bond_ratio * offset[component] / length * projected
            parts[component] = parts[component] + spring * summand
    return jnp.stack(parts)


def diagonal(stiff_pad):
    stiff_centre = inner_view(stiff_pad, 0, 0, 0)
    parts = [jnp.zeros_like(stiff_centre) for component in range(3)]
    for offset in neighbour_offsets:
        length = offset[0] * offset[0] + offset[1] * offset[1] + offset[2] * offset[2]
        spring = (
            0.5 * (stiff_centre + inner_view(stiff_pad, offset[0], offset[1], offset[2])) / length
        )
        for component in range(3):
            parts[component] = parts[component] + spring * (
                1.0 + bond_ratio * offset[component] * offset[component] / length
            )
    return jnp.stack(parts)


def local_solve(residual_ext, stiff_rim, diag_ext):
    widths = [(0, 0)] * (residual_ext.ndim - 3) + [(1, 1)] * 3
    solution = relax * residual_ext / diag_ext
    for sweep in range(SWEEPS - 1):
        solution = (
            solution
            + relax * (residual_ext - spring_force(jnp.pad(solution, widths), stiff_rim)) / diag_ext
        )
    return solution


def cross(first, second):
    return jnp.stack(
        [
            first[1] * second[2] - first[2] * second[1],
            first[2] * second[0] - first[0] * second[2],
            first[0] * second[1] - first[1] * second[0],
        ]
    )


def local_coords(size_x, size_y, size_z):
    along_x = ((2.0 * jnp.arange(size_x, dtype=jnp.float32) + 1.0) / size_x - 1.0).reshape(
        size_x, 1, 1
    )
    along_y = ((2.0 * jnp.arange(size_y, dtype=jnp.float32) + 1.0) / size_y - 1.0).reshape(
        1, size_y, 1
    )
    along_z = ((2.0 * jnp.arange(size_z, dtype=jnp.float32) + 1.0) / size_z - 1.0).reshape(
        1, 1, size_z
    )
    return (along_x, along_y, along_z)


def fold_axis(spread, axis):
    size = spread.shape[axis]
    count = size - 4
    inner = lax.slice_in_dim(spread, 2, size - 2, axis=axis)
    lower = lax.slice_in_dim(spread, 0, 1, axis=axis)
    upper = lax.slice_in_dim(spread, size - 1, size, axis=axis)
    head = lax.slice_in_dim(inner, 0, 1, axis=axis) + lower
    tail = lax.slice_in_dim(inner, count - 1, count, axis=axis) + upper
    middle = lax.slice_in_dim(inner, 1, count - 1, axis=axis)
    return jnp.concatenate([head, middle, tail], axis=axis)


def body(right_side, phase_labels, phase_moduli, coarse_nodes, coarse_inverse):
    phases = phase_moduli.shape[0]
    matches = phase_labels[None] == jnp.arange(phases, dtype=jnp.int32)[:, None, None, None]
    coarse_stiff = jnp.sum(jnp.where(matches, phase_moduli[:, None, None, None], 0.0), axis=0)
    stiffness = jnp.repeat(jnp.repeat(jnp.repeat(coarse_stiff, 2, axis=0), 2, axis=1), 2, axis=2)
    stiff_rim = extended(stiffness, (("gx", 0), ("gy", 1), ("gz", 2)), 2)
    diag_ext = diagonal(stiff_rim)
    stiff_near = stiff_rim[1:-1, 1:-1, 1:-1]
    size_x, size_y, size_z = stiffness.shape
    coords = local_coords(size_x, size_y, size_z)
    node_count = coarse_inverse.shape[0] // 6
    onehot = (
        jnp.arange(node_count, dtype=jnp.int32)[:, None] == coarse_nodes.reshape(1, -1)
    ).astype(jnp.float32)

    def accumulate(piece):
        return jnp.dot(coarse_inverse, piece, precision=highest)

    def coarse_part(residual):
        moments = jnp.concatenate([residual, cross(coords, residual)], axis=0).reshape(6, -1)
        node_sums = jnp.einsum("gc,mc->gm", onehot, moments, precision=highest).reshape(-1)
        solved = accumulate(lax.all_gather(node_sums, ("gx", "gy", "gz"), axis=0, tiled=True))
        per_cell = jnp.einsum("gm,gc->mc", solved.reshape(node_count, 6), onehot, precision=highest)
        per_cell = per_cell.reshape(6, size_x, size_y, size_z)
        return per_cell[:3] + cross(per_cell[3:], coords)

    def local_part(residual_ext):
        solution = local_solve(residual_ext, stiff_rim, diag_ext)
        spread = extended(solution, (("gx", 1), ("gy", 2), ("gz", 3)), 1)
        return fold_axis(fold_axis(fold_axis(spread, 1), 2), 3)

    def widen(vector):
        return extended(vector, (("gx", 1), ("gy", 2), ("gz", 3)), 1)

    def precondition(residual_form):
        return local_part(widen(residual_form)) + coarse_part(residual_form)

    residual = right_side
    solution_field = jnp.zeros_like(right_side)

    def global_sum(value):
        return lax.psum(value, ("gx", "gy", "gz"))

    search = precondition(residual)
    norm_now = global_sum(jnp.sum(residual * search))
    direction = search
    for step in range(ITERS):
        image = spring_force(widen(direction), stiff_near)
        step_size = norm_now / global_sum(jnp.sum(direction * image))
        solution_field = solution_field + step_size * direction
        residual = residual - step_size * image
        if step + 1 < ITERS:
            search = precondition(residual)
            norm_next = global_sum(jnp.sum(residual * search))
            direction = search + norm_next / norm_now * direction
            norm_now = norm_next
    return (solution_field, residual)


def solution(mesh):
    in_specs = (
        P(None, "gx", "gy", "gz"),
        P("gx", "gy", "gz"),
        P(),
        P("gx", "gy", "gz"),
        P(("gx", "gy", "gz"), None),
    )
    out_specs = (P(None, "gx", "gy", "gz"), P(None, "gx", "gy", "gz"))
    return jax.shard_map(body, mesh=mesh, in_specs=in_specs, out_specs=out_specs, check_vma=False)
```

profile of v0, /device:TPU:1, one launch (start us, length us, event | category | flops | bytes accessed | tf_op | source)
XLA Modules:
  0.0 682.7 jit_solution(17536681381676741998)
XLA Ops:
  1.8 9.8 %collective-permute-start.6 = (f32[2,8,128]{2,1,0:T(8,128)S(1)}, f32[2,8,128]{2,1,0:T(8,128)S(1)}, u32[]{:S(2)}, u32[]{:S(2)}) collective-permute-start(f32[2,8,128]{2,1,0:T(8,128)S(1)} %broadcast_in_dim.51), channel_id=1, source_target_pairs={{0,32},{32,64},{64,96},{96,128},{128,160},{160,192},{192,224},{1,3... | collective-permute-start | bytes 24584 | tf_op jit(solution)/shard_map/ppermute | solution.py:29
  13.8 7.9 %collective-permute-start = (f32[3,1,8,128]{3,2,1,0:T(8,128)S(1)}, f32[3,1,8,128]{3,2,1,0:T(8,128)S(1)}, u32[]{:S(2)}, u32[]{:S(2)}) collective-permute-start(f32[3,1,8,128]{3,2,1,0:T(8,128)S(1)} %get-tuple-element.274), channel_id=1, source_target_pairs={{0,32},{32,64},{64,96},{96,128},{128,160},{160,192},{192,224},{1,3... | collective-permute-start | bytes 36872 | tf_op jit(solution)/shard_map/ppermute | solution.py:29
  26.5 79.8 %all-reduce.6 = f32[9216]{0:T(1024)S(1)} all-reduce(f32[9216]{0:T(1024)S(1)} %dynamic-update-slice), channel_id=1, replica_groups=mesh['gx'=8,'gy'=8,'gz'=4] {'gx','gy','gz'}, use_global_device_ids=true, to_apply=%add.6 | all-reduce | flops 9216 | bytes 73728
  128.4 4.3 collective-permute-start.4
  136.1 4.1 collective-permute-done.5
  159.1 5.2 collective-permute-start.12
  166.0 7.6 %collective-permute-done.13 = f32[3,1,10,130]{3,2,1,0:T(8,128)S(1)} collective-permute-done((f32[3,1,10,130]{3,2,1,0:T(8,128)S(1)}, f32[3,1,10,130]{3,2,1,0:T(8,128)S(1)}, u32[]{:S(2)}, u32[]{:S(2)}) %collective-permute-start.13) | collective-permute-done | bytes 15632 | tf_op jit(solution)/shard_map/ppermute | solution.py:30
  190.9 4.1 collective-permute-done.17
  197.7 5.2 collective-permute-start.18
  204.2 7.5 %collective-permute-done.19 = f32[3,1,8,128]{3,2,1,0:T(8,128)S(1)} collective-permute-done((f32[3,1,8,128]{3,2,1,0:T(8,128)S(1)}, f32[3,1,8,128]{3,2,1,0:T(8,128)S(1)}, u32[]{:S(2)}, u32[]{:S(2)}) %collective-permute-start.19) | collective-permute-done | bytes 12320 | tf_op jit(solution)/shard_map/ppermute | solution.py:30
  211.7 5.1 collective-permute-start.20
  226.5 6.0 collective-permute-done.23
  240.8 74.1 %all-reduce.8 = (f32[]{:T(128)}, f32[]{:T(128)}) all-reduce(f32[]{:T(128)} %get-tuple-element.29, f32[]{:T(128)} %fusion.1595), channel_id=1, replica_groups=mesh['gx'=8,'gy'=8,'gz'=4] {'gx','gy','gz'}, use_global_device_ids=true, to_apply=%region_2.3 | all-reduce | flops 2 | bytes 16 | tf_op jit(solution)/shard_map/psum | solution.py:170
  319.5 4.6 collective-permute-start.24
  330.7 77.3 %all-reduce.7 = f32[9216]{0:T(1024)} all-reduce(f32[9216]{0:T(1024)} %dynamic-update-slice.1), channel_id=1, replica_groups=mesh['gx'=8,'gy'=8,'gz'=4] {'gx','gy','gz'}, use_global_device_ids=true, to_apply=%add.7 | all-reduce | flops 9216 | bytes 73728
  410.2 4.2 collective-permute-start.26
  457.0 7.2 %collective-permute-done.31 = f32[3,1,10,130]{3,2,1,0:T(8,128)S(1)} collective-permute-done((f32[3,1,10,130]{3,2,1,0:T(8,128)S(1)}, f32[3,1,10,130]{3,2,1,0:T(8,128)S(1)}, u32[]{:S(2)}, u32[]{:S(2)}) %collective-permute-start.31) | collective-permute-done | bytes 15632 | tf_op jit(solution)/shard_map/ppermute | solution.py:30
  464.2 4.6 collective-permute-start.32
  482.0 4.1 collective-permute-done.35
  488.8 75.1 %psum.30 = f32[]{:T(128)} all-reduce(f32[]{:T(128)} %get-tuple-element.18), channel_id=1, replica_groups=mesh['gx'=8,'gy'=8,'gz'=4] {'gx','gy','gz'}, use_global_device_ids=true, to_apply=%region_6.7 | all-reduce | flops 1 | bytes 8 | tf_op jit(solution)/shard_map/psum | solution.py:170
  565.2 5.2 collective-permute-start.36
  571.7 7.0 %collective-permute-done.37 = f32[3,1,8,128]{3,2,1,0:T(8,128)S(1)} collective-permute-done((f32[3,1,8,128]{3,2,1,0:T(8,128)S(1)}, f32[3,1,8,128]{3,2,1,0:T(8,128)S(1)}, u32[]{:S(2)}, u32[]{:S(2)}) %collective-permute-start.37) | collective-permute-done | bytes 12320 | tf_op jit(solution)/shard_map/ppermute | solution.py:30
  591.7 6.0 collective-permute-done.41
  606.7 73.8 %psum.31 = f32[]{:T(128)} all-reduce(f32[]{:T(128)} %fusion.1594), channel_id=1, replica_groups=mesh['gx'=8,'gy'=8,'gz'=4] {'gx','gy','gz'}, use_global_device_ids=true, to_apply=%region_8.9 | all-reduce | flops 1 | bytes 8 | tf_op jit(solution)/shard_map/psum | solution.py:170
  (507 shorter events, 185.2 us)
Async XLA Ops:
  1.8 107.3 %collective-permute-start.6 = (f32[2,8,128]{2,1,0:T(8,128)S(1)}, f32[2,8,128]{2,1,0:T(8,128)S(1)}, u32[]{:S(2)}, u32[]{:S(2)}) collective-permute-start(f32[2,8,128]{2,1,0:T(8,128)S(1)} %broadcast_in_dim.51), channel_id=1, source_target_pairs={{0,32},{32,64},{64,96},{96,128},{128,160},{160,192},{192,224},{1,3... | collective-permute-start | bytes 24584 | tf_op jit(solution)/shard_map/ppermute | solution.py:29
  11.7 97.4 %collective-permute-start.7 = (f32[2,8,128]{2,1,0:T(8,128)S(1)}, f32[2,8,128]{2,1,0:T(8,128)S(1)}, u32[]{:S(2)}, u32[]{:S(2)}) collective-permute-start(f32[2,8,128]{2,1,0:T(8,128)S(1)} %broadcast_in_dim.59), channel_id=1, source_target_pairs={{32,0},{64,32},{96,64},{128,96},{160,128},{192,160},{224,192},{33,... | collective-permute-start | bytes 24584 | tf_op jit(solution)/shard_map/ppermute | solution.py:30
  13.8 100.5 %collective-permute-start = (f32[3,1,8,128]{3,2,1,0:T(8,128)S(1)}, f32[3,1,8,128]{3,2,1,0:T(8,128)S(1)}, u32[]{:S(2)}, u32[]{:S(2)}) collective-permute-start(f32[3,1,8,128]{3,2,1,0:T(8,128)S(1)} %get-tuple-element.274), channel_id=1, source_target_pairs={{0,32},{32,64},{64,96},{96,128},{128,160},{160,192},{192,224},{1,3... | collective-permute-start | bytes 36872 | tf_op jit(solution)/shard_map/ppermute | solution.py:29
  21.6 92.7 %collective-permute-start.1 = (f32[3,1,8,128]{3,2,1,0:T(8,128)S(1)}, f32[3,1,8,128]{3,2,1,0:T(8,128)S(1)}, u32[]{:S(2)}, u32[]{:S(2)}) collective-permute-start(f32[3,1,8,128]{3,2,1,0:T(8,128)S(1)} %get-tuple-element.273), channel_id=1, source_target_pairs={{32,0},{64,32},{96,64},{128,96},{160,128},{192,160},{224,192},{33,... | collective-permute-start | bytes 36872 | tf_op jit(solution)/shard_map/ppermute | solution.py:30
  117.5 7.8 %collective-permute-start.10 = (f32[12,12,2]{2,1,0:T(8,128)S(1)}, f32[12,12,2]{2,1,0:T(8,128)S(1)}, u32[]{:S(2)}, u32[]{:S(2)}) collective-permute-start(f32[12,12,2]{2,1,0:T(8,128)S(1)} %get-tuple-element.271), channel_id=1, source_target_pairs={{0,1},{1,2},{2,3},{4,5},{5,6},{6,7},{8,9},{9,10},{10,11},{12,13},{... | collective-permute-start | bytes 3464 | tf_op jit(solution)/shard_map/ppermute | solution.py:29
  128.4 7.7 %collective-permute-start.4 = (f32[3,10,10,1]{3,0,2,1:T(4,128)S(1)}, f32[3,10,10,1]{3,0,2,1:T(4,128)S(1)}, u32[]{:S(2)}, u32[]{:S(2)}) collective-permute-start(f32[3,10,10,1]{3,0,2,1:T(4,128)S(1)} %get-tuple-element.241), channel_id=1, source_target_pairs={{0,1},{1,2},{2,3},{4,5},{5,6},{6,7},{8,9},{9,10},{10,11},{12,13},{... | collective-permute-start | bytes 3608 | tf_op jit(solution)/shard_map/ppermute | solution.py:29
  132.7 7.5 %collective-permute-start.5 = (f32[3,10,10,1]{3,0,2,1:T(4,128)S(1)}, f32[3,10,10,1]{3,0,2,1:T(4,128)S(1)}, u32[]{:S(2)}, u32[]{:S(2)}) collective-permute-start(f32[3,10,10,1]{3,0,2,1:T(4,128)S(1)} %get-tuple-element.242), channel_id=1, source_target_pairs={{1,0},{2,1},{3,2},{5,4},{6,5},{7,6},{9,8},{10,9},{11,10},{13,12},{... | collective-permute-start | bytes 3608 | tf_op jit(solution)/shard_map/ppermute | solution.py:30
  164.3 9.3 %collective-permute-start.13 = (f32[3,1,10,130]{3,2,1,0:T(8,128)S(1)}, f32[3,1,10,130]{3,2,1,0:T(8,128)S(1)}, u32[]{:S(2)}, u32[]{:S(2)}) collective-permute-start(f32[3,1,10,130]{3,2,1,0:T(8,128)S(1)} %get-tuple-element.108), channel_id=1, source_target_pairs={{32,0},{64,32},{96,64},{128,96},{160,128},{192,160},{224,192},{33,... | collective-permute-start | bytes 46808 | tf_op jit(solution)/shard_map/ppermute | solution.py:30
  183.3 7.6 %collective-permute-start.16 = (f32[3,12,12,1]{3,2,1,0:T(8,128)S(1)}, f32[3,12,12,1]{3,2,1,0:T(8,128)S(1)}, u32[]{:S(2)}, u32[]{:S(2)}) collective-permute-start(f32[3,12,12,1]{3,2,1,0:T(8,128)S(1)} %get-tuple-element.101), channel_id=1, source_target_pairs={{0,1},{1,2},{2,3},{4,5},{5,6},{6,7},{8,9},{9,10},{10,11},{12,13},{... | collective-permute-start | bytes 5192 | tf_op jit(solution)/shard_map/ppermute | solution.py:29
  185.8 9.2 %collective-permute-start.17 = (f32[3,12,12,1]{3,2,1,0:T(8,128)S(1)}, f32[3,12,12,1]{3,2,1,0:T(8,128)S(1)}, u32[]{:S(2)}, u32[]{:S(2)}) collective-permute-start(f32[3,12,12,1]{3,2,1,0:T(8,128)S(1)} %get-tuple-element.102), channel_id=1, source_target_pairs={{1,0},{2,1},{3,2},{5,4},{6,5},{7,6},{9,8},{10,9},{11,10},{13,12},{... | collective-permute-start | bytes 5192 | tf_op jit(solution)/shard_map/ppermute | solution.py:30
  202.9 8.8 %collective-permute-start.19 = (f32[3,1,8,128]{3,2,1,0:T(8,128)S(1)}, f32[3,1,8,128]{3,2,1,0:T(8,128)S(1)}, u32[]{:S(2)}, u32[]{:S(2)}) collective-permute-start(f32[3,1,8,128]{3,2,1,0:T(8,128)S(1)} %get-tuple-element.270), channel_id=1, source_target_pairs={{32,0},{64,32},{96,64},{128,96},{160,128},{192,160},{224,192},{33,... | collective-permute-start | bytes 36872 | tf_op jit(solution)/shard_map/ppermute | solution.py:30
  211.7 7.1 %collective-permute-start.20 = (f32[3,10,1,128]{3,2,1,0:T(1,128)S(1)}, f32[3,10,1,128]{3,2,1,0:T(1,128)S(1)}, u32[]{:S(2)}, u32[]{:S(2)}) collective-permute-start(f32[3,10,1,128]{3,2,1,0:T(1,128)S(1)} %get-tuple-element.255), channel_id=1, source_target_pairs={{0,4},{4,8},{8,12},{12,16},{16,20},{20,24},{24,28},{1,5},{5,9},{9,... | collective-permute-start | bytes 46088 | tf_op jit(solution)/shard_map/ppermute | solution.py:29
  222.2 12.9 %collective-permute-start.22 = (f32[3,10,10,1]{3,0,2,1:T(4,128)S(1)}, f32[3,10,10,1]{3,0,2,1:T(4,128)S(1)}, u32[]{:S(2)}, u32[]{:S(2)}) collective-permute-start(f32[3,10,10,1]{3,0,2,1:T(4,128)S(1)} %get-tuple-element.239), channel_id=1, source_target_pairs={{0,1},{1,2},{2,3},{4,5},{5,6},{6,7},{8,9},{9,10},{10,11},{12,13},{... | collective-permute-start | bytes 3608 | tf_op jit(solution)/shard_map/ppermute | solution.py:29
  225.0 7.5 %collective-permute-start.23 = (f32[3,10,10,1]{3,0,2,1:T(4,128)S(1)}, f32[3,10,10,1]{3,0,2,1:T(4,128)S(1)}, u32[]{:S(2)}, u32[]{:S(2)}) collective-permute-start(f32[3,10,10,1]{3,0,2,1:T(4,128)S(1)} %get-tuple-element.240), channel_id=1, source_target_pairs={{1,0},{2,1},{3,2},{5,4},{6,5},{7,6},{9,8},{10,9},{11,10},{13,12},{... | collective-permute-start | bytes 3608 | tf_op jit(solution)/shard_map/ppermute | solution.py:30
  319.5 88.4 %collective-permute-start.24 = (f32[3,1,8,128]{3,2,1,0:T(8,128)}, f32[3,1,8,128]{3,2,1,0:T(8,128)}, u32[]{:S(2)}, u32[]{:S(2)}) collective-permute-start(f32[3,1,8,128]{3,2,1,0:T(8,128)} %get-tuple-element.267), channel_id=1, source_target_pairs={{0,32},{32,64},{64,96},{96,128},{128,160},{160,192},{192,224},{1,3... | collective-permute-start | bytes 36872 | tf_op jit(solution)/shard_map/ppermute | solution.py:29
  324.2 83.8 %collective-permute-start.25 = (f32[3,1,8,128]{3,2,1,0:T(8,128)}, f32[3,1,8,128]{3,2,1,0:T(8,128)}, u32[]{:S(2)}, u32[]{:S(2)}) collective-permute-start(f32[3,1,8,128]{3,2,1,0:T(8,128)} %get-tuple-element.268), channel_id=1, source_target_pairs={{32,0},{64,32},{96,64},{128,96},{160,128},{192,160},{224,192},{33,... | collective-permute-start | bytes 36872 | tf_op jit(solution)/shard_map/ppermute | solution.py:30
  410.2 10.2 %collective-permute-start.26 = (f32[3,10,1,128]{3,2,1,0:T(1,128)}, f32[3,10,1,128]{3,2,1,0:T(1,128)}, u32[]{:S(2)}, u32[]{:S(2)}) collective-permute-start(f32[3,10,1,128]{3,2,1,0:T(1,128)} %get-tuple-element.252), channel_id=1, source_target_pairs={{0,4},{4,8},{8,12},{12,16},{16,20},{20,24},{24,28},{1,5},{5,9},{9,... | collective-permute-start | bytes 46088 | tf_op jit(solution)/shard_map/ppermute | solution.py:29
  426.4 7.5 %collective-permute-start.29 = (f32[3,10,10,1]{3,0,2,1:T(4,128)S(1)}, f32[3,10,10,1]{3,0,2,1:T(4,128)S(1)}, u32[]{:S(2)}, u32[]{:S(2)}) collective-permute-start(f32[3,10,10,1]{3,0,2,1:T(4,128)S(1)} %get-tuple-element.238), channel_id=1, source_target_pairs={{1,0},{2,1},{3,2},{5,4},{6,5},{7,6},{9,8},{10,9},{11,10},{13,12},{... | collective-permute-start | bytes 3608 | tf_op jit(solution)/shard_map/ppermute | solution.py:30
  454.8 9.4 %collective-permute-start.31 = (f32[3,1,10,130]{3,2,1,0:T(8,128)S(1)}, f32[3,1,10,130]{3,2,1,0:T(8,128)S(1)}, u32[]{:S(2)}, u32[]{:S(2)}) collective-permute-start(f32[3,1,10,130]{3,2,1,0:T(8,128)S(1)} %get-tuple-element.106), channel_id=1, source_target_pairs={{32,0},{64,32},{96,64},{128,96},{160,128},{192,160},{224,192},{33,... | collective-permute-start | bytes 46808 | tf_op jit(solution)/shard_map/ppermute | solution.py:30
  474.4 7.6 %collective-permute-start.34 = (f32[3,12,12,1]{3,2,1,0:T(8,128)S(1)}, f32[3,12,12,1]{3,2,1,0:T(8,128)S(1)}, u32[]{:S(2)}, u32[]{:S(2)}) collective-permute-start(f32[3,12,12,1]{3,2,1,0:T(8,128)S(1)} %get-tuple-element.97), channel_id=1, source_target_pairs={{0,1},{1,2},{2,3},{4,5},{5,6},{6,7},{8,9},{9,10},{10,11},{12,13},{... | collective-permute-start | bytes 5192 | tf_op jit(solution)/shard_map/ppermute | solution.py:29
  476.9 9.2 %collective-permute-start.35 = (f32[3,12,12,1]{3,2,1,0:T(8,128)S(1)}, f32[3,12,12,1]{3,2,1,0:T(8,128)S(1)}, u32[]{:S(2)}, u32[]{:S(2)}) collective-permute-start(f32[3,12,12,1]{3,2,1,0:T(8,128)S(1)} %get-tuple-element.98), channel_id=1, source_target_pairs={{1,0},{2,1},{3,2},{5,4},{6,5},{7,6},{9,8},{10,9},{11,10},{13,12},{... | collective-permute-start | bytes 5192 | tf_op jit(solution)/shard_map/ppermute | solution.py:30
  570.4 8.3 %collective-permute-start.37 = (f32[3,1,8,128]{3,2,1,0:T(8,128)S(1)}, f32[3,1,8,128]{3,2,1,0:T(8,128)S(1)}, u32[]{:S(2)}, u32[]{:S(2)}) collective-permute-start(f32[3,1,8,128]{3,2,1,0:T(8,128)S(1)} %get-tuple-element.266), channel_id=1, source_target_pairs={{32,0},{64,32},{96,64},{128,96},{160,128},{192,160},{224,192},{33,... | collective-permute-start | bytes 36872 | tf_op jit(solution)/shard_map/ppermute | solution.py:30
  587.7 12.7 %collective-permute-start.40 = (f32[3,10,10,1]{3,0,2,1:T(4,128)S(1)}, f32[3,10,10,1]{3,0,2,1:T(4,128)S(1)}, u32[]{:S(2)}, u32[]{:S(2)}) collective-permute-start(f32[3,10,10,1]{3,0,2,1:T(4,128)S(1)} %get-tuple-element.235), channel_id=1, source_target_pairs={{0,1},{1,2},{2,3},{4,5},{5,6},{6,7},{8,9},{9,10},{10,11},{12,13},{... | collective-permute-start | bytes 3608 | tf_op jit(solution)/shard_map/ppermute | solution.py:29
  590.1 7.5 %collective-permute-start.41 = (f32[3,10,10,1]{3,0,2,1:T(4,128)S(1)}, f32[3,10,10,1]{3,0,2,1:T(4,128)S(1)}, u32[]{:S(2)}, u32[]{:S(2)}) collective-permute-start(f32[3,10,10,1]{3,0,2,1:T(4,128)S(1)} %get-tuple-element.236), channel_id=1, source_target_pairs={{1,0},{2,1},{3,2},{5,4},{6,5},{7,6},{9,8},{10,9},{11,10},{13,12},{... | collective-permute-start | bytes 3608 | tf_op jit(solution)/shard_map/ppermute | solution.py:30
  (148 other events, 1792.6 us)
where the time goes:
time: 690 us; the launch traced here: 683 us
  blocking collectives  380 us (55%)
  starting transfers between devices  120 us (17%)
  waiting for transfers between devices  85.4 us (12%)
  other arithmetic  64 us (9%)
  local copies, waits for them, and re-layouts  16 us (2%)
  matrix products  9.04 us (1%)
  between operations  7.75 us (1%)
    psum x3, blocking collectives, global_sum(): return lax.psum(value, ('gx', 'gy', 'gz'))  223 us
    unnamed x2, blocking collectives  157 us
    ppermute x21, starting transfers between devices, extended(): before = lax.ppermute(last, axis, up)  87.8 us
    ppermute x21, waiting for transfers between devices, extended(): after = lax.ppermute(leading, axis, down)  76 us
    ppermute x21, starting transfers between devices, extended(): after = lax.ppermute(leading, axis, down)  32.7 us
    another operation x18, other arithmetic, spring_force(): return jnp.stack(parts)  32.1 us
    concatenate x27, other arithmetic, extended(): x = jnp.concatenate([before, x, after], axis=dim)  15.2 us
  transfers between devices with their start and end apart: 42, of which 21 were waited for; matrix products, arithmetic and copies ran while one was open for 4% of the time, Pallas kernels for 0%

commit v1 on v0

--- a/solution.py
+++ b/solution.py
@@ -2,6 +2,7 @@
 import jax.numpy as jnp
 from jax import lax
 from jax.sharding import PartitionSpec as P
+from jax.lax import psum
 
 SWEEPS = 4
 ITERS = 2
@@ -167,7 +168,7 @@
     solution_field = jnp.zeros_like(right_side)
 
     def global_sum(value):
-        return lax.psum(value, ("gx", "gy", "gz"))
+        return psum(psum(value, "gx"), ("gy", "gz"))
 
     search = precondition(residual)
     norm_now = global_sum(jnp.sum(residual * search))

time: 690 us -> 752 us (1.090)
  blocking collectives: 380 us -> 433 us
    psum x3 -> x6, blocking collectives: 223 us -> 272 us  [global_sum(): return psum(psum(value, 'gx'), ('gy', 'gz'))]
where the time goes in v1:
time: 752 us; the launch traced here: 739 us
  blocking collectives  433 us (58%)
  starting transfers between devices  126 us (17%)
  waiting for transfers between devices  83.6 us (11%)
  other arithmetic  63.9 us (8%)
  local copies, waits for them, and re-layouts  16 us (2%)
  matrix products  9.02 us (1%)
  between operations  7.73 us (1%)
    psum x6, blocking collectives, global_sum(): return psum(psum(value, 'gx'), ('gy', 'gz'))  272 us
    unnamed x2, blocking collectives  161 us
    ppermute x21, starting transfers between devices, extended(): before = lax.ppermute(last, axis, up)  86.5 us
    ppermute x21, waiting for transfers between devices, extended(): after = lax.ppermute(leading, axis, down)  74.2 us
    ppermute x21, starting transfers between devices, extended(): after = lax.ppermute(leading, axis, down)  39.6 us
    another operation x18, other arithmetic, spring_force(): return jnp.stack(parts)  32.1 us
    concatenate x27, other arithmetic, extended(): x = jnp.concatenate([before, x, after], axis=dim)  15.2 us
  transfers between devices with their start and end apart: 42, of which 21 were waited for; matrix products, arithmetic and copies ran while one was open for 4% of the time, Pallas kernels for 0%

profile of v1, /device:TPU:1, one launch (start us, length us, event | category | flops | bytes accessed | tf_op | source)
XLA Modules:
  0.0 739.0 jit_solution(1192415692491690265)
XLA Ops:
  1.8 9.8 %collective-permute-start.6 = (f32[2,8,128]{2,1,0:T(8,128)S(1)}, f32[2,8,128]{2,1,0:T(8,128)S(1)}, u32[]{:S(2)}, u32[]{:S(2)}) collective-permute-start(f32[2,8,128]{2,1,0:T(8,128)S(1)} %broadcast_in_dim.51), channel_id=1, source_target_pairs={{0,32},{32,64},{64,96},{96,128},{128,160},{160,192},{192,224},{1,3... | collective-permute-start | bytes 24584 | tf_op jit(solution)/shard_map/ppermute | solution.py:30
  13.8 7.9 %collective-permute-start = (f32[3,1,8,128]{3,2,1,0:T(8,128)S(1)}, f32[3,1,8,128]{3,2,1,0:T(8,128)S(1)}, u32[]{:S(2)}, u32[]{:S(2)}) collective-permute-start(f32[3,1,8,128]{3,2,1,0:T(8,128)S(1)} %get-tuple-element.276), channel_id=1, source_target_pairs={{0,32},{32,64},{64,96},{96,128},{128,160},{160,192},{192,224},{1,3... | collective-permute-start | bytes 36872 | tf_op jit(solution)/shard_map/ppermute | solution.py:30
  26.5 79.8 %all-reduce.6 = f32[9216]{0:T(1024)S(1)} all-reduce(f32[9216]{0:T(1024)S(1)} %dynamic-update-slice), channel_id=1, replica_groups=mesh['gx'=8,'gy'=8,'gz'=4] {'gx','gy','gz'}, use_global_device_ids=true, to_apply=%add.6 | all-reduce | flops 9216 | bytes 73728
  128.4 4.3 collective-permute-start.4
  159.1 5.2 collective-permute-start.12
  166.0 7.6 %collective-permute-done.13 = f32[3,1,10,130]{3,2,1,0:T(8,128)S(1)} collective-permute-done((f32[3,1,10,130]{3,2,1,0:T(8,128)S(1)}, f32[3,1,10,130]{3,2,1,0:T(8,128)S(1)}, u32[]{:S(2)}, u32[]{:S(2)}) %collective-permute-start.13) | collective-permute-done | bytes 15632 | tf_op jit(solution)/shard_map/ppermute | solution.py:31
  197.7 5.2 collective-permute-start.18
  204.2 7.5 %collective-permute-done.19 = f32[3,1,8,128]{3,2,1,0:T(8,128)S(1)} collective-permute-done((f32[3,1,8,128]{3,2,1,0:T(8,128)S(1)}, f32[3,1,8,128]{3,2,1,0:T(8,128)S(1)}, u32[]{:S(2)}, u32[]{:S(2)}) %collective-permute-start.19) | collective-permute-done | bytes 12320 | tf_op jit(solution)/shard_map/ppermute | solution.py:31
  211.7 5.1 collective-permute-start.20
  226.5 6.0 collective-permute-done.23
  240.8 24.7 %all-reduce.9 = (f32[]{:T(128)}, f32[]{:T(128)}) all-reduce(f32[]{:T(128)} %get-tuple-element.31, f32[]{:T(128)} %fusion.1595), channel_id=1, replica_groups=mesh['gx'=8,'gy'=8,'gz'=4] {'gx'}, use_global_device_ids=true, to_apply=%region_2.3 | all-reduce | flops 2 | bytes 16 | tf_op jit(solution)/shard_map/psum | solution.py:171
  265.5 64.9 %all-reduce.8 = (f32[]{:T(128)}, f32[]{:T(128)}) all-reduce(f32[]{:T(128)} %get-tuple-element.14, f32[]{:T(128)} %get-tuple-element.15), channel_id=1, replica_groups=mesh['gx'=8,'gy'=8,'gz'=4] {'gy','gz'}, use_global_device_ids=true, to_apply=%region_3.4 | all-reduce | flops 2 | bytes 16 | tf_op jit(solution)/shard_map/psum | solution.py:171
  335.0 4.4 collective-permute-start.24
  345.9 81.3 %all-reduce.7 = f32[9216]{0:T(1024)} all-reduce(f32[9216]{0:T(1024)} %dynamic-update-slice.1), channel_id=1, replica_groups=mesh['gx'=8,'gy'=8,'gz'=4] {'gx','gy','gz'}, use_global_device_ids=true, to_apply=%add.7 | all-reduce | flops 9216 | bytes 73728
  470.2 5.6 collective-permute-start.30
  477.9 7.2 collective-permute-done.31
  503.0 4.1 collective-permute-done.35
  509.8 24.7 %psum.60 = f32[]{:T(128)} all-reduce(f32[]{:T(128)} %get-tuple-element.20), channel_id=1, replica_groups=mesh['gx'=8,'gy'=8,'gz'=4] {'gx'}, use_global_device_ids=true, to_apply=%region_8.9 | all-reduce | flops 1 | bytes 8 | tf_op jit(solution)/shard_map/psum | solution.py:171
  534.5 65.5 %psum.61 = f32[]{:T(128)} all-reduce(f32[]{:T(128)} %psum.60), channel_id=1, replica_groups=mesh['gx'=8,'gy'=8,'gz'=4] {'gy','gz'}, use_global_device_ids=true, to_apply=%region_9.10 | all-reduce | flops 1 | bytes 8 | tf_op jit(solution)/shard_map/psum | solution.py:171
  605.9 7.0 collective-permute-done.37
  614.9 8.9 %collective-permute-start.39 = (f32[3,10,1,128]{3,2,1,0:T(1,128)S(1)}, f32[3,10,1,128]{3,2,1,0:T(1,128)S(1)}, u32[]{:S(2)}, u32[]{:S(2)}) collective-permute-start(f32[3,10,1,128]{3,2,1,0:T(1,128)S(1)} %get-tuple-element.252), channel_id=1, source_target_pairs={{4,0},{8,4},{12,8},{16,12},{20,16},{24,20},{28,24},{5,1},{9,5},{13... | collective-permute-start | bytes 46088 | tf_op jit(solution)/shard_map/ppermute | solution.py:31
  629.6 6.4 collective-permute-done.41
  645.1 24.4 %psum.62 = f32[]{:T(128)} all-reduce(f32[]{:T(128)} %fusion.1594), channel_id=1, replica_groups=mesh['gx'=8,'gy'=8,'gz'=4] {'gx'}, use_global_device_ids=true, to_apply=%region_11.12 | all-reduce | flops 1 | bytes 8 | tf_op jit(solution)/shard_map/psum | solution.py:171
  669.6 67.3 %psum.63 = f32[]{:T(128)} all-reduce(f32[]{:T(128)} %psum.62), channel_id=1, replica_groups=mesh['gx'=8,'gy'=8,'gz'=4] {'gy','gz'}, use_global_device_ids=true, to_apply=%region_12.13 | all-reduce | flops 1 | bytes 8 | tf_op jit(solution)/shard_map/psum | solution.py:171
  (510 shorter events, 196.4 us)
Async XLA Ops:
  1.8 107.3 %collective-permute-start.6 = (f32[2,8,128]{2,1,0:T(8,128)S(1)}, f32[2,8,128]{2,1,0:T(8,128)S(1)}, u32[]{:S(2)}, u32[]{:S(2)}) collective-permute-start(f32[2,8,128]{2,1,0:T(8,128)S(1)} %broadcast_in_dim.51), channel_id=1, source_target_pairs={{0,32},{32,64},{64,96},{96,128},{128,160},{160,192},{192,224},{1,3... | collective-permute-start | bytes 24584 | tf_op jit(solution)/shard_map/ppermute | solution.py:30
  11.7 97.4 %collective-permute-start.7 = (f32[2,8,128]{2,1,0:T(8,128)S(1)}, f32[2,8,128]{2,1,0:T(8,128)S(1)}, u32[]{:S(2)}, u32[]{:S(2)}) collective-permute-start(f32[2,8,128]{2,1,0:T(8,128)S(1)} %broadcast_in_dim.59), channel_id=1, source_target_pairs={{32,0},{64,32},{96,64},{128,96},{160,128},{192,160},{224,192},{33,... | collective-permute-start | bytes 24584 | tf_op jit(solution)/shard_map/ppermute | solution.py:31
  13.8 100.5 %collective-permute-start = (f32[3,1,8,128]{3,2,1,0:T(8,128)S(1)}, f32[3,1,8,128]{3,2,1,0:T(8,128)S(1)}, u32[]{:S(2)}, u32[]{:S(2)}) collective-permute-start(f32[3,1,8,128]{3,2,1,0:T(8,128)S(1)} %get-tuple-element.276), channel_id=1, source_target_pairs={{0,32},{32,64},{64,96},{96,128},{128,160},{160,192},{192,224},{1,3... | collective-permute-start | bytes 36872 | tf_op jit(solution)/shard_map/ppermute | solution.py:30
  21.6 92.7 %collective-permute-start.1 = (f32[3,1,8,128]{3,2,1,0:T(8,128)S(1)}, f32[3,1,8,128]{3,2,1,0:T(8,128)S(1)}, u32[]{:S(2)}, u32[]{:S(2)}) collective-permute-start(f32[3,1,8,128]{3,2,1,0:T(8,128)S(1)} %get-tuple-element.275), channel_id=1, source_target_pairs={{32,0},{64,32},{96,64},{128,96},{160,128},{192,160},{224,192},{33,... | collective-permute-start | bytes 36872 | tf_op jit(solution)/shard_map/ppermute | solution.py:31
  117.4 7.8 %collective-permute-start.10 = (f32[12,12,2]{2,1,0:T(8,128)S(1)}, f32[12,12,2]{2,1,0:T(8,128)S(1)}, u32[]{:S(2)}, u32[]{:S(2)}) collective-permute-start(f32[12,12,2]{2,1,0:T(8,128)S(1)} %get-tuple-element.273), channel_id=1, source_target_pairs={{0,1},{1,2},{2,3},{4,5},{5,6},{6,7},{8,9},{9,10},{10,11},{12,13},{... | collective-permute-start | bytes 3464 | tf_op jit(solution)/shard_map/ppermute | solution.py:30
  128.4 7.7 %collective-permute-start.4 = (f32[3,10,10,1]{3,0,2,1:T(4,128)S(1)}, f32[3,10,10,1]{3,0,2,1:T(4,128)S(1)}, u32[]{:S(2)}, u32[]{:S(2)}) collective-permute-start(f32[3,10,10,1]{3,0,2,1:T(4,128)S(1)} %get-tuple-element.243), channel_id=1, source_target_pairs={{0,1},{1,2},{2,3},{4,5},{5,6},{6,7},{8,9},{9,10},{10,11},{12,13},{... | collective-permute-start | bytes 3608 | tf_op jit(solution)/shard_map/ppermute | solution.py:30
  132.7 7.5 %collective-permute-start.5 = (f32[3,10,10,1]{3,0,2,1:T(4,128)S(1)}, f32[3,10,10,1]{3,0,2,1:T(4,128)S(1)}, u32[]{:S(2)}, u32[]{:S(2)}) collective-permute-start(f32[3,10,10,1]{3,0,2,1:T(4,128)S(1)} %get-tuple-element.244), channel_id=1, source_target_pairs={{1,0},{2,1},{3,2},{5,4},{6,5},{7,6},{9,8},{10,9},{11,10},{13,12},{... | collective-permute-start | bytes 3608 | tf_op jit(solution)/shard_map/ppermute | solution.py:31
  164.3 9.3 %collective-permute-start.13 = (f32[3,1,10,130]{3,2,1,0:T(8,128)S(1)}, f32[3,1,10,130]{3,2,1,0:T(8,128)S(1)}, u32[]{:S(2)}, u32[]{:S(2)}) collective-permute-start(f32[3,1,10,130]{3,2,1,0:T(8,128)S(1)} %get-tuple-element.110), channel_id=1, source_target_pairs={{32,0},{64,32},{96,64},{128,96},{160,128},{192,160},{224,192},{33,... | collective-permute-start | bytes 46808 | tf_op jit(solution)/shard_map/ppermute | solution.py:31
  183.3 7.6 %collective-permute-start.16 = (f32[3,12,12,1]{3,2,1,0:T(8,128)S(1)}, f32[3,12,12,1]{3,2,1,0:T(8,128)S(1)}, u32[]{:S(2)}, u32[]{:S(2)}) collective-permute-start(f32[3,12,12,1]{3,2,1,0:T(8,128)S(1)} %get-tuple-element.103), channel_id=1, source_target_pairs={{0,1},{1,2},{2,3},{4,5},{5,6},{6,7},{8,9},{9,10},{10,11},{12,13},{... | collective-permute-start | bytes 5192 | tf_op jit(solution)/shard_map/ppermute | solution.py:30
  185.8 9.2 %collective-permute-start.17 = (f32[3,12,12,1]{3,2,1,0:T(8,128)S(1)}, f32[3,12,12,1]{3,2,1,0:T(8,128)S(1)}, u32[]{:S(2)}, u32[]{:S(2)}) collective-permute-start(f32[3,12,12,1]{3,2,1,0:T(8,128)S(1)} %get-tuple-element.104), channel_id=1, source_target_pairs={{1,0},{2,1},{3,2},{5,4},{6,5},{7,6},{9,8},{10,9},{11,10},{13,12},{... | collective-permute-start | bytes 5192 | tf_op jit(solution)/shard_map/ppermute | solution.py:31
  202.9 8.8 %collective-permute-start.19 = (f32[3,1,8,128]{3,2,1,0:T(8,128)S(1)}, f32[3,1,8,128]{3,2,1,0:T(8,128)S(1)}, u32[]{:S(2)}, u32[]{:S(2)}) collective-permute-start(f32[3,1,8,128]{3,2,1,0:T(8,128)S(1)} %get-tuple-element.272), channel_id=1, source_target_pairs={{32,0},{64,32},{96,64},{128,96},{160,128},{192,160},{224,192},{33,... | collective-permute-start | bytes 36872 | tf_op jit(solution)/shard_map/ppermute | solution.py:31
  222.1 12.9 %collective-permute-start.22 = (f32[3,10,10,1]{3,0,2,1:T(4,128)S(1)}, f32[3,10,10,1]{3,0,2,1:T(4,128)S(1)}, u32[]{:S(2)}, u32[]{:S(2)}) collective-permute-start(f32[3,10,10,1]{3,0,2,1:T(4,128)S(1)} %get-tuple-element.241), channel_id=1, source_target_pairs={{0,1},{1,2},{2,3},{4,5},{5,6},{6,7},{8,9},{9,10},{10,11},{12,13},{... | collective-permute-start | bytes 3608 | tf_op jit(solution)/shard_map/ppermute | solution.py:30
  335.0 92.2 %collective-permute-start.24 = (f32[3,1,8,128]{3,2,1,0:T(8,128)}, f32[3,1,8,128]{3,2,1,0:T(8,128)}, u32[]{:S(2)}, u32[]{:S(2)}) collective-permute-start(f32[3,1,8,128]{3,2,1,0:T(8,128)} %get-tuple-element.269), channel_id=1, source_target_pairs={{0,32},{32,64},{64,96},{96,128},{128,160},{160,192},{192,224},{1,3... | collective-permute-start | bytes 36872 | tf_op jit(solution)/shard_map/ppermute | solution.py:30
  339.4 87.8 %collective-permute-start.25 = (f32[3,1,8,128]{3,2,1,0:T(8,128)}, f32[3,1,8,128]{3,2,1,0:T(8,128)}, u32[]{:S(2)}, u32[]{:S(2)}) collective-permute-start(f32[3,1,8,128]{3,2,1,0:T(8,128)} %get-tuple-element.270), channel_id=1, source_target_pairs={{32,0},{64,32},{96,64},{128,96},{160,128},{192,160},{224,192},{33,... | collective-permute-start | bytes 36872 | tf_op jit(solution)/shard_map/ppermute | solution.py:31
  429.4 10.1 %collective-permute-start.26 = (f32[3,10,1,128]{3,2,1,0:T(1,128)}, f32[3,10,1,128]{3,2,1,0:T(1,128)}, u32[]{:S(2)}, u32[]{:S(2)}) collective-permute-start(f32[3,10,1,128]{3,2,1,0:T(1,128)} %get-tuple-element.254), channel_id=1, source_target_pairs={{0,4},{4,8},{8,12},{12,16},{16,20},{20,24},{24,28},{1,5},{5,9},{9,... | collective-permute-start | bytes 46088 | tf_op jit(solution)/shard_map/ppermute | solution.py:30
  470.2 7.8 %collective-permute-start.30 = (f32[3,1,10,130]{3,2,1,0:T(8,128)S(1)}, f32[3,1,10,130]{3,2,1,0:T(8,128)S(1)}, u32[]{:S(2)}, u32[]{:S(2)}) collective-permute-start(f32[3,1,10,130]{3,2,1,0:T(8,128)S(1)} %get-tuple-element.107), channel_id=1, source_target_pairs={{0,32},{32,64},{64,96},{96,128},{128,160},{160,192},{192,224},{1,3... | collective-permute-start | bytes 46808 | tf_op jit(solution)/shard_map/ppermute | solution.py:30
  475.8 9.4 %collective-permute-start.31 = (f32[3,1,10,130]{3,2,1,0:T(8,128)S(1)}, f32[3,1,10,130]{3,2,1,0:T(8,128)S(1)}, u32[]{:S(2)}, u32[]{:S(2)}) collective-permute-start(f32[3,1,10,130]{3,2,1,0:T(8,128)S(1)} %get-tuple-element.108), channel_id=1, source_target_pairs={{32,0},{64,32},{96,64},{128,96},{160,128},{192,160},{224,192},{33,... | collective-permute-start | bytes 46808 | tf_op jit(solution)/shard_map/ppermute | solution.py:31
  494.5 8.5 %collective-permute-start.34 = (f32[3,12,12,1]{3,2,1,0:T(8,128)S(1)}, f32[3,12,12,1]{3,2,1,0:T(8,128)S(1)}, u32[]{:S(2)}, u32[]{:S(2)}) collective-permute-start(f32[3,12,12,1]{3,2,1,0:T(8,128)S(1)} %get-tuple-element.99), channel_id=1, source_target_pairs={{0,1},{1,2},{2,3},{4,5},{5,6},{6,7},{8,9},{9,10},{10,11},{12,13},{... | collective-permute-start | bytes 5192 | tf_op jit(solution)/shard_map/ppermute | solution.py:30
  497.9 9.2 %collective-permute-start.35 = (f32[3,12,12,1]{3,2,1,0:T(8,128)S(1)}, f32[3,12,12,1]{3,2,1,0:T(8,128)S(1)}, u32[]{:S(2)}, u32[]{:S(2)}) collective-permute-start(f32[3,12,12,1]{3,2,1,0:T(8,128)S(1)} %get-tuple-element.100), channel_id=1, source_target_pairs={{1,0},{2,1},{3,2},{5,4},{6,5},{7,6},{9,8},{10,9},{11,10},{13,12},{... | collective-permute-start | bytes 5192 | tf_op jit(solution)/shard_map/ppermute | solution.py:31
  604.6 8.3 %collective-permute-start.37 = (f32[3,1,8,128]{3,2,1,0:T(8,128)S(1)}, f32[3,1,8,128]{3,2,1,0:T(8,128)S(1)}, u32[]{:S(2)}, u32[]{:S(2)}) collective-permute-start(f32[3,1,8,128]{3,2,1,0:T(8,128)S(1)} %get-tuple-element.268), channel_id=1, source_target_pairs={{32,0},{64,32},{96,64},{128,96},{160,128},{192,160},{224,192},{33,... | collective-permute-start | bytes 36872 | tf_op jit(solution)/shard_map/ppermute | solution.py:31
  613.0 10.8 %collective-permute-start.38 = (f32[3,10,1,128]{3,2,1,0:T(1,128)S(1)}, f32[3,10,1,128]{3,2,1,0:T(1,128)S(1)}, u32[]{:S(2)}, u32[]{:S(2)}) collective-permute-start(f32[3,10,1,128]{3,2,1,0:T(1,128)S(1)} %get-tuple-element.251), channel_id=1, source_target_pairs={{0,4},{4,8},{8,12},{12,16},{16,20},{20,24},{24,28},{1,5},{5,9},{9,... | collective-permute-start | bytes 46088 | tf_op jit(solution)/shard_map/ppermute | solution.py:30
  614.9 9.7 %collective-permute-start.39 = (f32[3,10,1,128]{3,2,1,0:T(1,128)S(1)}, f32[3,10,1,128]{3,2,1,0:T(1,128)S(1)}, u32[]{:S(2)}, u32[]{:S(2)}) collective-permute-start(f32[3,10,1,128]{3,2,1,0:T(1,128)S(1)} %get-tuple-element.252), channel_id=1, source_target_pairs={{4,0},{8,4},{12,8},{16,12},{20,16},{24,20},{28,24},{5,1},{9,5},{13... | collective-permute-start | bytes 46088 | tf_op jit(solution)/shard_map/ppermute | solution.py:31
  624.8 14.0 %collective-permute-start.40 = (f32[3,10,10,1]{3,0,2,1:T(4,128)S(1)}, f32[3,10,10,1]{3,0,2,1:T(4,128)S(1)}, u32[]{:S(2)}, u32[]{:S(2)}) collective-permute-start(f32[3,10,10,1]{3,0,2,1:T(4,128)S(1)} %get-tuple-element.237), channel_id=1, source_target_pairs={{0,1},{1,2},{2,3},{4,5},{5,6},{6,7},{8,9},{9,10},{10,11},{12,13},{... | collective-permute-start | bytes 3608 | tf_op jit(solution)/shard_map/ppermute | solution.py:30
  628.1 7.9 %collective-permute-start.41 = (f32[3,10,10,1]{3,0,2,1:T(4,128)S(1)}, f32[3,10,10,1]{3,0,2,1:T(4,128)S(1)}, u32[]{:S(2)}, u32[]{:S(2)}) collective-permute-start(f32[3,10,10,1]{3,0,2,1:T(4,128)S(1)} %get-tuple-element.238), channel_id=1, source_target_pairs={{1,0},{2,1},{3,2},{5,4},{6,5},{7,6},{9,8},{10,9},{11,10},{13,12},{... | collective-permute-start | bytes 3608 | tf_op jit(solution)/shard_map/ppermute | solution.py:31
  (148 other events, 1804.4 us)
